TPU v7x, 32 devices: a whole 2x2x4 slice. The times are simulated.
32 devices in a mesh: rows: 16 (over z, x, core), mlp: 2 (over y).
Axes of the slice: x: 2, y: 2, z: 4, core: 2. Of those that a mesh axis runs over, the one named last changes fastest.
Arguments:
- node_rows: bfloat16 [16384, 512], P(('rows', 'mlp')), may hold values from -6 to 6
- noise_cond: bfloat16 [8, 128], replicated, may hold values from -6 to 6
- sample_id: int32 [16384], P(('rows', 'mlp')), may hold values from 0 to 7, as said below
- neighbours: int32 [16384, 16], P(('rows', 'mlp')), may hold values from 0 to 16383, as said below
- ada_weight: bfloat16 [128, 2048], replicated, may hold values from -0.25 to 0.25
- ada_bias: bfloat16 [2048], replicated, may hold values from -3 to 3
- query_weight: bfloat16 [512, 512], replicated, may hold values from -0.25 to 0.25
- keyval_weight: bfloat16 [512, 1024], replicated, may hold values from -0.25 to 0.25
- out_weight: bfloat16 [512, 512], replicated, may hold values from -0.5 to 0.5
- up_weight: bfloat16 [512, 2048], P(None, 'mlp'), may hold values from -0.25 to 0.25
- up_bias: bfloat16 [2048], P('mlp'), may hold values from -3 to 3
- down_weight: bfloat16 [2048, 512], P('mlp'), may hold values from -0.125 to 0.125
- down_bias: bfloat16 [512], replicated, may hold values from -3 to 3
- cotangent: bfloat16 [16384, 512], P(('rows', 'mlp')), may hold values from -6 to 6
Outputs:
- layer_out: bfloat16 [16384, 512], P(('rows', 'mlp'))
- grad_rows: float32 [16384, 512], P(('rows', 'mlp'))
- grad_cond: float32 [8, 128], replicated
- grad_ada_weight: float32 [128, 2048], replicated
- grad_ada_bias: float32 [2048], replicated
- grad_query_weight: float32 [512, 512], replicated
- grad_keyval_weight: float32 [512, 1024], replicated
- grad_out_weight: float32 [512, 512], replicated
- grad_up_weight: float32 [512, 2048], P(None, 'mlp')
- grad_up_bias: float32 [2048], P('mlp')
- grad_down_weight: float32 [2048, 512], P('mlp')
- grad_down_bias: float32 [512], replicated
Inputs may be any that keep to these rules, and one draw needn't show every extreme that they name: Row n stands for mesh node n // 8 of sample sample_id[n]. Each of its 16 neighbours is a row of the same sample whose node differs by at most 64, counted cyclically over the 2048 nodes; so it lies within 512 positions of n, counted cyclically over 16384. The first two are the rows of nodes one below and one above, cyclically. sample_id[n] depends only on n mod 8, and each sample is carried by 2048 rows.
All inputs are finite; a program needn't handle non-finite values.
Results may differ from a plain program's by a relative error of at most 0.012.
The roundings to bfloat16 on the way count: a program that leaves them out, or rounds other values in their place, can miss the bound.
Values may be sent and summed in bfloat16 or wider, within the bound.
A program may use at most 192 MiB of HBM per device.

v0:
```python
import math
import jax
import jax.numpy as jnp
from jax import lax
from jax.sharding import PartitionSpec as P

HEADS = 4
EPSILON = 1e-05
PRECISE = lax.Precision.HIGHEST


def with_halo(x, sides, width):
    for axis, dim in sides:
        peers, length = (lax.axis_size(axis), x.shape[dim])
        up = [(i, (i + 1) % peers) for i in range(peers)]
        down = [(j, i) for i, j in up]
        last = lax.slice_in_dim(x, length - width, length, axis=dim)
        leading = lax.slice_in_dim(x, 0, width, axis=dim)
        before = lax.ppermute(last, axis, up)
        after = lax.ppermute(leading, axis, down)
        x = jnp.concatenate([before, x, after], axis=dim)
    return x


def shifted(x, axis, by):
    peers = lax.axis_size(axis)
    return lax.ppermute(x, axis, [(i, (i + by) % peers) for i in range(peers)])


def layer_norm(values):
    centred = values - jnp.mean(values, axis=-1, keepdims=True)
    inverse = lax.rsqrt(jnp.mean(centred * centred, axis=-1, keepdims=True) + EPSILON)
    return (centred * inverse, inverse)


def norm_back(grad_norm, normed, inverse):
    return inverse * (
        grad_norm
        - jnp.mean(grad_norm, axis=-1, keepdims=True)
        - normed * jnp.mean(grad_norm * normed, axis=-1, keepdims=True)
    )


def bf_dot(left_operand, right_operand):
    return jnp.dot(left_operand, right_operand, preferred_element_type=jnp.float32)


def split_heads(picked, feature_width, head_count):
    row_total, near_count = (picked.shape[0], picked.shape[1])
    head_size = feature_width // head_count
    keys_near = picked[:, :, :feature_width].reshape(row_total, near_count, head_count, head_size)
    values_near = picked[:, :, feature_width:].reshape(row_total, near_count, head_count, head_size)
    return (keys_near, values_near)


def swish_back(grad_active, hidden):
    logistic = jax.nn.sigmoid(hidden)
    return (grad_active * logistic * (1.0 + hidden * (1.0 - logistic))).astype(jnp.bfloat16)


def shards(
    node_rows,
    noise_cond,
    sample_id,
    neighbours,
    ada_weight,
    ada_bias,
    query_weight,
    keyval_weight,
    out_weight,
    up_weight,
    up_bias,
    down_weight,
    down_bias,
    cotangent,
):
    row_count, feature_width = node_rows.shape
    head_count = HEADS
    head_size = feature_width // head_count
    near_count = neighbours.shape[1]
    factor = 1.0 / math.sqrt(head_size)
    samples = noise_cond.shape[0]
    devices = lax.axis_size(("rows", "mlp"))
    first_row = lax.axis_index(("rows", "mlp")) * row_count
    block_rows = min(row_count, 512)
    blocks = row_count // block_rows
    inputs = node_rows.astype(jnp.float32)
    modulation = bf_dot(noise_cond, ada_weight) + ada_bias.astype(jnp.float32)
    onehot = (sample_id[:, None] == jnp.arange(samples, dtype=jnp.int32)[None, :]).astype(
        jnp.float32
    )
    modrows = jnp.dot(onehot, modulation, precision=PRECISE)
    local_index = jnp.mod(neighbours - first_row + row_count, row_count * devices)
    index_blocks = local_index.reshape(blocks, block_rows, near_count)
    norm_one, inverse_one = layer_norm(inputs)
    normed_one = (
        norm_one * (1.0 + modrows[:, :feature_width])
        + modrows[:, feature_width : 2 * feature_width]
    ).astype(jnp.bfloat16)
    queries = bf_dot(normed_one, query_weight).astype(jnp.bfloat16)
    keyvals = bf_dot(normed_one, keyval_weight).astype(jnp.bfloat16)
    kv_table = with_halo(keyvals, ((("rows", "mlp"), 0),), row_count)

    def attend(block_items):
        query_part, index_part = block_items
        keys_near, values_near = split_heads(kv_table[index_part], feature_width, head_count)
        scores = (
            jnp.einsum("bhe,bjhe->bhj", query_part, keys_near, preferred_element_type=jnp.float32)
            * factor
        )
        highest = jnp.max(scores, axis=-1, keepdims=True)
        exponent = jnp.exp(scores - highest)
        denominator = jnp.sum(exponent, axis=-1, keepdims=True)
        attn_probs = (exponent / denominator).astype(jnp.bfloat16)
        mixture = jnp.einsum(
            "bhj,bjhe->bhe", attn_probs, values_near, preferred_element_type=jnp.float32
        )
        return (
            mixture.reshape(block_rows, feature_width).astype(jnp.bfloat16),
            (highest + jnp.log(denominator))[..., 0],
        )

    mixture, log_total = lax.map(
        attend, (queries.reshape(blocks, block_rows, head_count, head_size), index_blocks)
    )
    mixture = mixture.reshape(row_count, feature_width)
    middle = inputs + bf_dot(mixture, out_weight)
    norm_two, inverse_two = layer_norm(middle)
    normed_two = (
        norm_two * (1.0 + modrows[:, 2 * feature_width : 3 * feature_width])
        + modrows[:, 3 * feature_width :]
    ).astype(jnp.bfloat16)
    gathered = lax.all_gather(normed_two, "mlp", axis=0, tiled=True)
    hidden = bf_dot(gathered, up_weight) + up_bias.astype(jnp.float32)
    active = jax.nn.silu(hidden).astype(jnp.bfloat16)
    branch = lax.psum_scatter(bf_dot(active, down_weight), "mlp", scatter_dimension=0, tiled=True)
    layer_out = (middle + branch + down_bias.astype(jnp.float32)).astype(jnp.bfloat16)
    grad_out = cotangent.astype(jnp.float32)
    cot_rows = lax.all_gather(cotangent, "mlp", axis=0, tiled=True)
    grad_hidden = swish_back(bf_dot(cot_rows, down_weight.T), hidden)
    grad_two = lax.psum_scatter(
        bf_dot(grad_hidden, up_weight.T), "mlp", scatter_dimension=0, tiled=True
    )
    up_share = bf_dot(gathered.T, grad_hidden)
    upb_share = jnp.sum(grad_hidden.astype(jnp.float32), axis=0)
    down_share = bf_dot(active.T, cot_rows)
    grad_up, grad_upb, grad_down = lax.psum((up_share, upb_share, down_share), "rows")
    grad_middle = grad_out + norm_back(
        grad_two * (1.0 + modrows[:, 2 * feature_width : 3 * feature_width]), norm_two, inverse_two
    )
    grad_attended = grad_middle.astype(jnp.bfloat16)
    output_share = bf_dot(mixture.T, grad_attended)
    grad_mixture = bf_dot(grad_attended, out_weight.T).astype(jnp.bfloat16)
    queries_back = bf_dot(normed_one, query_weight).astype(jnp.bfloat16)
    table_back = with_halo(
        bf_dot(normed_one, keyval_weight).astype(jnp.bfloat16), ((("rows", "mlp"), 0),), row_count
    )

    def attend_back(table_grad, block_items):
        query_part, index_part, log_part, grad_part = block_items
        keys_near, values_near = split_heads(table_back[index_part], feature_width, head_count)
        scores = (
            jnp.einsum("bhe,bjhe->bhj", query_part, keys_near, preferred_element_type=jnp.float32)
            * factor
        )
        attn_exact = jnp.exp(scores - log_part[..., None])
        attn_probs = attn_exact.astype(jnp.bfloat16)
        grad_heads = grad_part.reshape(block_rows, head_count, head_size)
        grad_probs = jnp.einsum(
            "bhe,bjhe->bhj", grad_heads, values_near, preferred_element_type=jnp.float32
        )
        grad_scores = (
            attn_exact * (grad_probs - jnp.sum(attn_exact * grad_probs, axis=-1, keepdims=True))
        ).astype(jnp.bfloat16)
        grad_query = (
            jnp.einsum("bhj,bjhe->bhe", grad_scores, keys_near, preferred_element_type=jnp.float32)
            * factor
        )
        grad_keys = (
            jnp.einsum("bhj,bhe->bjhe", grad_scores, query_part, preferred_element_type=jnp.float32)
            * factor
        )
        grad_values = jnp.einsum(
            "bhj,bhe->bjhe", attn_probs, grad_heads, preferred_element_type=jnp.float32
        )
        grad_near = jnp.concatenate(
            [
                grad_keys.reshape(block_rows, near_count, feature_width),
                grad_values.reshape(block_rows, near_count, feature_width),
            ],
            axis=-1,
        )
        table_grad = table_grad.at[index_part.reshape(-1)].add(
            grad_near.reshape(block_rows * near_count, 2 * feature_width)
        )
        return (table_grad, grad_query.reshape(block_rows, feature_width).astype(jnp.bfloat16))

    table_grad, grad_queries = lax.scan(
        attend_back,
        jnp.zeros((3 * row_count, 2 * feature_width), jnp.float32),
        (
            queries_back.reshape(blocks, block_rows, head_count, head_size),
            index_blocks,
            log_total,
            grad_mixture.reshape(blocks, block_rows, feature_width),
        ),
    )
    grad_queries = grad_queries.reshape(row_count, feature_width)
    from_upper = shifted(table_grad[:row_count], ("rows", "mlp"), -1)
    from_lower = shifted(table_grad[2 * row_count :], ("rows", "mlp"), 1)
    grad_keyvals = (table_grad[row_count : 2 * row_count] + from_upper + from_lower).astype(
        jnp.bfloat16
    )
    query_share = bf_dot(normed_one.T, grad_queries)
    keyval_share = bf_dot(normed_one.T, grad_keyvals)
    grad_one = bf_dot(grad_queries, query_weight.T) + bf_dot(grad_keyvals, keyval_weight.T)
    grad_rows = grad_middle + norm_back(
        grad_one * (1.0 + modrows[:, :feature_width]), norm_one, inverse_one
    )
    grad_modrows = jnp.concatenate(
        [grad_one * norm_one, grad_one, grad_two * norm_two, grad_two], axis=1
    )
    modulation_share = jnp.dot(onehot.T, grad_modrows, precision=PRECISE)
    summed = lax.psum(
        (query_share, keyval_share, output_share, modulation_share, jnp.sum(grad_out, axis=0)),
        ("rows", "mlp"),
    )
    grad_query_weight, grad_keyval_weight, grad_out_weight, grad_modulation, grad_down_bias = summed
    grad_ada_weight = jnp.dot(noise_cond.astype(jnp.float32).T, grad_modulation, precision=PRECISE)
    grad_ada_bias = jnp.sum(grad_modulation, axis=0)
    grad_cond = jnp.dot(grad_modulation, ada_weight.astype(jnp.float32).T, precision=PRECISE)
    return (
        layer_out,
        grad_rows,
        grad_cond,
        grad_ada_weight,
        grad_ada_bias,
        grad_query_weight,
        grad_keyval_weight,
        grad_out_weight,
        grad_up,
        grad_upb,
        grad_down,
        grad_down_bias,
    )


def solution(mesh):
    placed = (
        P(("rows", "mlp"), None),
        P(),
        P(("rows", "mlp")),
        P(("rows", "mlp"), None),
        P(),
        P(),
        P(),
        P(),
        P(),
        P(None, "mlp"),
        P("mlp"),
        P("mlp", None),
        P(),
        P(("rows", "mlp"), None),
    )
    return jax.shard_map(
        shards,
        mesh=mesh,
        in_specs=placed,
        out_specs=(
            P(("rows", "mlp"), None),
            P(("rows", "mlp"), None),
            P(),
            P(),
            P(),
            P(),
            P(),
            P(),
            P(None, "mlp"),
            P("mlp"),
            P("mlp", None),
            P(),
        ),
        check_vma=False,
    )
```

profile of v0, /device:TPU:0, one launch (start us, length us, event | category | flops | bytes accessed | tf_op | source)
XLA Modules:
  0.0 817.2 jit_solution(563137369281137952)
XLA Ops:
  18.6 6.4 collective-permute-start.1
  26.5 29.8 %collective-permute-done.1 = bf16[512,1024]{1,0:T(8,128)(2,1)} collective-permute-done((bf16[512,1024]{1,0:T(8,128)(2,1)}, bf16[512,1024]{1,0:T(8,128)(2,1)}, u32[]{:S(2)}, u32[]{:S(2)}) %collective-permute-start.1) | collective-permute-done | bytes 1048608 | tf_op jit(solution)/shard_map/ppermute | solution.py:20
  60.4 42.8 %gather_fusion = bf16[8192,1024]{1,0:T(8,128)(2,1)} fusion(bf16[1536,1024]{1,0:T(8,128)(2,1)} %pad_maximum_fusion, s32[8192]{0:T(1024)S(1)} %broadcast_clamp_fusion), kind=kCustom, calls=%fused_computation | custom fusion | bytes 33587200 | tf_op jit(solution)/shard_map/while/body/eval_jaxpr/gather | solution.py:106
  103.2 18.5 %slice_bitcast_fusion.1 = (bf16[512,2,4,8,128]{4,3,2,1,0:T(8,128)(2,1)}, bf16[512,2,4,8,128]{4,3,2,1,0:T(8,128)(2,1)}, bf16[512,16,512]{2,1,0:T(8,128)(2,1)}, bf16[512,16,512]{2,1,0:T(8,128)(2,1)}) fusion(bf16[512,16,1024]{2,1,0:T(8,128)(2,1)} %bitcast.86), kind=kLoop, calls=%fused_computation.125 | loop fusion | bytes 50331648
  121.7 12.5 %reshape.162 = bf16[512,16,4,128]{3,2,1,0:T(4,128)(2,1)} reshape(bf16[512,16,512]{2,1,0:T(8,128)(2,1)} %get-tuple-element.104) | data formatting | bytes 16777216 | tf_op jit(solution)/shard_map/while/body/eval_jaxpr/reshape | solution.py:51
  134.2 12.9 %multiply_reduce_fusion.1 = f32[512,4,16]{1,2,0:T(8,128)} fusion(f32[512,4,128]{2,1,0:T(4,128)S(1)} %copy.76, bf16[512,16,4,128]{3,2,1,0:T(4,128)(2,1)} %reshape.162), kind=kLoop, calls=%fused_computation.10 | loop fusion | flops 12550144 | bytes 9568256
  151.0 5.7 fusion.8
  161.5 31.9 %all-gather.3.cloned.1.call-done = bf16[1024,512]{1,0:T(8,128)(2,1)} async-done(((bf16[512,512]{1,0:T(8,128)(2,1)}), bf16[1024,512]{1,0:T(8,128)(2,1)}) %all-gather.3.cloned.1.call-update) | async-done | bytes 1048592 | tf_op jit(solution)/shard_map/all_gather | solution.py:133
  193.4 5.5 multiply_convert_fusion.1
  198.9 17.4 %all-gather.5.cloned.1.call-done = bf16[1024,512]{1,0:T(8,128)(2,1)} async-done(((bf16[512,512]{1,0:T(8,128)(2,1)}), bf16[1024,512]{1,0:T(8,128)(2,1)}) %all-gather.5.cloned.1.call-update) | async-done | bytes 1048592 | tf_op jit(solution)/shard_map/all_gather | solution.py:139
  233.9 12.6 %reshape.163 = bf16[512,16,4,128]{3,2,1,0:T(4,128)(2,1)} reshape(bf16[512,16,512]{2,1,0:T(8,128)(2,1)} %get-tuple-element.105) | data formatting | bytes 16777216 | tf_op jit(solution)/shard_map/while/body/eval_jaxpr/reshape | solution.py:52
  246.5 10.8 %reduce-scatter.5.cloned.1.call-done = f32[512,512]{1,0:T(8,128)} async-done(((f32[1024,512]{1,0:T(8,128)}), f32[512,512]{1,0:T(8,128)}) %reduce-scatter.5.cloned.1.call-update) | async-done | bytes 1048592 | tf_op jit(solution)/shard_map/reduce_scatter | solution.py:141
  259.3 32.7 %reduce-scatter.3.cloned.1.call-done = f32[512,512]{1,0:T(8,128)} async-done(((f32[1024,512]{1,0:T(8,128)}), f32[512,512]{1,0:T(8,128)}) %reduce-scatter.3.cloned.1.call-update) | async-done | bytes 1048592 | tf_op jit(solution)/shard_map/reduce_scatter | solution.py:136
  299.2 24.5 %broadcast_multiply_fusion = (f32[512,4,128,16]{2,1,3,0:T(4,128)}, f32[512,4,16]{1,2,0:T(8,128)}) fusion(f32[512,4,128]{2,1,0:T(4,128)S(1)} %copy.77, f32[512,4,16]{1,2,0:T(8,128)} %copy.50, bf16[512,16,4,128]{3,2,1,0:T(4,128)(2,1)} %reshape.163), kind=kLoop, calls=%fused_computation.18 | loop fusion | flops 16744448 | bytes 26476544 | tf_op jit(solution)/shard_map/while/body/eval_jaxpr/bhj,bhe->bjhe/dot_general | solution.py:183
  323.7 12.7 %copy.114 = f32[1024,8,4,128]{3,1,2,0:T(8,128)} copy(f32[1024,8,4,128]{3,2,1,0:T(4,128)} %bitcast.88) | data formatting | bytes 33554432
  342.5 11.0 %multiply_multiply_fusion = f32[512,4,128,16]{2,1,3,0:T(4,128)S(1)} fusion(f32[512,4,128]{2,1,0:T(4,128)S(1)} %copy-done.7, f32[512,4,16]{1,2,0:T(8,128)} %copy.48), kind=kLoop, calls=%fused_computation.11 | loop fusion | flops 8388608 | bytes 17956864 | tf_op jit(solution)/shard_map/while/body/eval_jaxpr/mul | solution.py:180
  353.5 7.2 copy.115
  360.7 72.1 %scatter_custom_fusion = f32[1536,1024]{1,0:T(8,128)} fusion(s32[8192]{0:T(1024)S(1)} %bitcast.100, f32[8192,512]{1,0:T(8,128)} %bitcast.87, f32[]{:T(128)} %constant.96.clone.1, f32[8192,512]{1,0:T(8,128)} %bitcast.89, f32[]{:T(128)} %constant.55.clone.1), kind=kCustom, calls=%fused_computation.3 | custom fusion | flops 16777216 | bytes 39845896 | tf_op jit(solution)/shard_map/while/body/eval_jaxpr/scatter-add | solution.py:193
  442.1 5.8 fusion.5
  451.5 56.3 %collective-permute-done.2 = f32[512,1024]{1,0:T(8,128)} collective-permute-done((f32[512,1024]{1,0:T(8,128)}, f32[512,1024]{1,0:T(8,128)}, u32[]{:S(2)}, u32[]{:S(2)}) %collective-permute-start.2) | collective-permute-done | bytes 2097184 | tf_op jit(solution)/shard_map/ppermute | solution.py:27
  523.6 57.1 %psum.61 = f32[1024]{0:T(1024)} all-reduce(f32[1024]{0:T(1024)S(1)} %get-tuple-element.123), channel_id=1, replica_groups=mesh['rows'=16,'mlp'=2] {'rows'}, use_global_device_ids=true, to_apply=%region_21.22 | all-reduce | flops 1024 | bytes 8192 | tf_op jit(solution)/shard_map/psum | solution.py:147
  580.7 37.3 %psum.63 = f32[512]{0:T(512)} all-reduce(f32[512]{0:T(512)S(1)} %get-tuple-element.115), channel_id=1, replica_groups=mesh['rows'=16,'mlp'=2] {'rows','mlp'}, use_global_device_ids=true, to_apply=%region_24.25 | all-reduce | flops 512 | bytes 4096 | tf_op jit(solution)/shard_map/psum | solution.py:224
  618.0 67.5 %all-reduce.5.cloned.1.call-done = (f32[8,2048]{1,0:T(8,128)}, f32[512,512]{1,0:T(8,128)}, f32[512,1024]{1,0:T(8,128)}, f32[512,512]{1,0:T(8,128)}) async-done(((f32[8,2048]{1,0:T(8,128)}, f32[512,512]{1,0:T(8,128)}, f32[512,1024]{1,0:T(8,128)}, f32[512,512]{1,0:T(8,128)}), (f32[8,2048]{1,0:T(8,128)}, f32[512,512]{1,0:T(8,128)}, f32[512,1024]{1,0:T(8,128)}, ...) | async-done | bytes 4259856 | tf_op jit(solution)/shard_map/psum | solution.py:224
  692.0 108.9 %all-reduce.7.cloned.1.call-done = (f32[512,1024]{1,0:T(8,128)}, f32[1024,512]{1,0:T(8,128)}) async-done(((f32[512,1024]{1,0:T(8,128)}, f32[1024,512]{1,0:T(8,128)}), (f32[512,1024]{1,0:T(8,128)}, f32[1024,512]{1,0:T(8,128)})) %all-reduce.7.cloned.1.call-update) | async-done | bytes 4194320 | tf_op jit(solution)/shard_map/psum | solution.py:147
  (156 shorter events, 102.4 us)
Async XLA Ops:
  7.2 186.2 %copy-start = (bf16[512,1024]{1,0:T(8,128)(2,1)S(1)}, bf16[512,1024]{1,0:T(8,128)(2,1)}, u32[]{:S(2)}) copy-start(bf16[512,1024]{1,0:T(8,128)(2,1)} %param.23) | copy-start | bytes 3145732
  7.2 9.4 %copy-start.5 = (bf16[512,512]{1,0:T(8,128)(2,1)S(1)}, bf16[512,512]{1,0:T(8,128)(2,1)}, u32[]{:S(2)}) copy-start(bf16[512,512]{1,0:T(8,128)(2,1)} %param.14) | copy-start | bytes 1572868
  7.2 186.2 %all-gather.3.cloned.1.call-start = ((), (), s32[]{:S(2)}) async-start(), calls=%async_computation.2 | async-start | bytes 1572864 | tf_op jit(solution)/shard_map/all_gather | solution.py:133
  10.0 8.6 %copy-start.26 = (f32[512]{0:T(512)}, f32[512]{0:T(512)S(1)}, u32[]{:S(2)}) copy-start(f32[512]{0:T(512)S(1)} %add_rsqrt_fusion.1) | copy-start | bytes 6148
  12.0 13.4 %copy-start.28 = (s32[512,16]{0,1:T(8,128)S(1)}, s32[512,16]{0,1:T(8,128)}, u32[]{:S(2)}) copy-start(s32[512,16]{0,1:T(8,128)} %param.17) | copy-start | bytes 98308
  16.6 9.1 %copy-start.16 = (bf16[512,512]{1,0:T(8,128)(2,1)S(1)}, bf16[512,512]{1,0:T(8,128)(2,1)}, u32[]{:S(2)}) copy-start(bf16[512,512]{1,0:T(8,128)(2,1)} %param.20) | copy-start | bytes 1572868
  16.9 9.2 %copy-start.8 = (bf16[512,512]{1,0:T(8,128)(2,1)}, bf16[512,512]{1,0:T(8,128)(2,1)S(1)}, u32[]{:S(2)}) copy-start(bf16[512,512]{1,0:T(8,128)(2,1)S(1)} %fusion.32) | copy-start | bytes 1572868
  18.6 37.7 %collective-permute-start.1 = (bf16[512,1024]{1,0:T(8,128)(2,1)}, bf16[512,1024]{1,0:T(8,128)(2,1)}, u32[]{:S(2)}, u32[]{:S(2)}) collective-permute-start(bf16[512,1024]{1,0:T(8,128)(2,1)} %convolution_convert_fusion), channel_id=1, source_target_pairs={{1,0},{2,1},{3,2},{4,3},{5,4},{6,5},{7,6},{8,7},{9,8},{10,9},{11,1... | collective-permute-start | bytes 3145736 | tf_op jit(solution)/shard_map/ppermute | solution.py:20
  25.0 32.2 %collective-permute-start = (bf16[512,1024]{1,0:T(8,128)(2,1)}, bf16[512,1024]{1,0:T(8,128)(2,1)}, u32[]{:S(2)}, u32[]{:S(2)}) collective-permute-start(bf16[512,1024]{1,0:T(8,128)(2,1)} %convolution_convert_fusion), channel_id=1, source_target_pairs={{0,1},{1,2},{2,3},{3,4},{4,5},{5,6},{6,7},{7,8},{8,9},{9,10},{10,1... | collective-permute-start | bytes 3145736 | tf_op jit(solution)/shard_map/ppermute | solution.py:19
  26.4 107.8 %copy-start.6 = (f32[512,4,128]{2,1,0:T(4,128)}, f32[512,4,128]{2,1,0:T(4,128)S(1)}, u32[]{:S(2)}) copy-start(f32[512,4,128]{2,1,0:T(4,128)S(1)} %copy.76) | copy-start | bytes 3145732
  160.1 56.2 %all-gather.5.cloned.1.call-start = ((), (), s32[]{:S(2)}) async-start(), calls=%async_computation.4 | async-start | bytes 1572864 | tf_op jit(solution)/shard_map/all_gather | solution.py:139
  160.8 96.5 %reduce-scatter.5.cloned.1.call-start = ((), (), s32[]{:S(2)}) async-start(), calls=%async_computation.5 | async-start | bytes 3145728 | tf_op jit(solution)/shard_map/reduce_scatter | solution.py:141
  225.3 66.6 %reduce-scatter.3.cloned.1.call-start = ((), (), s32[]{:S(2)}) async-start(), calls=%async_computation.3 | async-start | bytes 3145728 | tf_op jit(solution)/shard_map/reduce_scatter | solution.py:136
  229.8 455.6 %all-reduce.5.cloned.1.call-start = ((), (), s32[]{:S(2)}) async-start(), calls=%async_computation.6 | async-start | bytes 8519680 | tf_op jit(solution)/shard_map/psum | solution.py:224
  437.6 70.2 %collective-permute-start.2 = (f32[512,1024]{1,0:T(8,128)}, f32[512,1024]{1,0:T(8,128)}, u32[]{:S(2)}, u32[]{:S(2)}) collective-permute-start(f32[512,1024]{1,0:T(8,128)} %get-tuple-element.106), channel_id=1, source_target_pairs={{0,31},{1,0},{2,1},{3,2},{4,3},{5,4},{6,5},{7,6},{8,7},{9,8},{10,9... | collective-permute-start | bytes 6291464 | tf_op jit(solution)/shard_map/ppermute | solution.py:27
  441.3 66.5 %collective-permute-start.3 = (f32[512,1024]{1,0:T(8,128)}, f32[512,1024]{1,0:T(8,128)}, u32[]{:S(2)}, u32[]{:S(2)}) collective-permute-start(f32[512,1024]{1,0:T(8,128)} %get-tuple-element.107), channel_id=1, source_target_pairs={{0,1},{1,2},{2,3},{3,4},{4,5},{5,6},{6,7},{7,8},{8,9},{9,10},{10,1... | collective-permute-start | bytes 6291464 | tf_op jit(solution)/shard_map/ppermute | solution.py:27
  451.5 61.8 %copy-start.4 = (f32[512,2048]{1,0:T(8,128)S(1)}, f32[512,2048]{1,0:T(8,128)}, u32[]{:S(2)}) copy-start(f32[512,2048]{1,0:T(8,128)} %copy-done.2) | copy-start | bytes 12582916
  451.5 61.8 %copy-start.22 = (bf16[512,1024]{1,0:T(8,128)(2,1)S(1)}, bf16[512,1024]{1,0:T(8,128)(2,1)}, u32[]{:S(2)}) copy-start(bf16[512,1024]{1,0:T(8,128)(2,1)} %param.21) | copy-start | bytes 3145732
  451.5 61.8 %copy-start.25 = (f32[512]{0:T(512)S(1)}, f32[512]{0:T(512)}, u32[]{:S(2)}) copy-start(f32[512]{0:T(512)} %copy-done.24) | copy-start | bytes 6148
  451.5 61.8 %copy-start.27 = (f32[512]{0:T(512)S(1)}, f32[512]{0:T(512)}, u32[]{:S(2)}) copy-start(f32[512]{0:T(512)} %copy-done.26) | copy-start | bytes 6148
  518.3 282.6 %all-reduce.7.cloned.1.call-start = ((), (), s32[]{:S(2)}) async-start(), calls=%async_computation.7 | async-start | bytes 8388608 | tf_op jit(solution)/shard_map/psum | solution.py:147
  521.0 165.9 %copy-start.29 = (bf16[8,128]{1,0:T(8,128)(2,1)S(1)}, bf16[8,128]{1,0:T(8,128)(2,1)}, u32[]{:S(2)}) copy-start(bf16[8,128]{1,0:T(8,128)(2,1)} %param.15) | copy-start | bytes 6148
  523.6 166.5 %copy-start.11 = (bf16[128,2048]{1,0:T(8,128)(2,1)S(1)}, bf16[128,2048]{1,0:T(8,128)(2,1)}, u32[]{:S(2)}) copy-start(bf16[128,2048]{1,0:T(8,128)(2,1)} %param.18) | copy-start | bytes 1572868
  688.8 117.7 %copy-start.20 = (f32[512,512]{1,0:T(8,128)S(1)}, f32[512,512]{1,0:T(8,128)}, u32[]{:S(2)}) copy-start(f32[512,512]{1,0:T(8,128)} %get-tuple-element.134) | copy-start | bytes 3145732
  (21 other events, 84.3 us)
Sparse Core Ops, SparseCore 0:
  160.2 33.1 all-gather.2
  194.9 21.2 all-gather.4
  225.4 31.8 reduce-scatter.4
  260.0 31.8 reduce-scatter.2
  518.4 166.9 all-reduce.4
  690.6 110.2 all-reduce.6
where the time goes:
time: 822 us; the launch traced here: 817 us
  waiting for transfers between devices  357 us (43%)
  local copies, waits for them, and re-layouts  143 us (17%)
  other arithmetic  142 us (17%)
  blocking collectives  94.4 us (11%)
  matrix products  55.4 us (7%)
  between operations  15 us (2%)
  starting transfers between devices  11.4 us (1%)
    psum x1, waiting for transfers between devices, shards(): lax.psum((up_share, upb_share, down_share), 'rows')  109 us
    scatter-add x1, other arithmetic, attend_back(): table_grad.at[index_part.reshape(-1)]  72.1 us
    psum x1, waiting for transfers between devices, shards(): lax.psum((query_share, keyval_share, output_share, modulation_share, jnp....  67.5 us
    psum x1, blocking collectives, shards(): lax.psum((up_share, upb_share, down_share), 'rows')  57.1 us
    ppermute x2, waiting for transfers between devices, shifted(): return lax.ppermute(x, axis, [(i, (i + by) % peers) for i in range(peers)])  56.3 us
    unnamed x81, local copies, waits for them, and re-layouts  55.4 us
    gather x1, local copies, waits for them, and re-layouts, attend(): kv_table[index_part]  42.8 us
    psum x1, blocking collectives, shards(): lax.psum((query_share, keyval_share, output_share, modulation_share, jnp....  37.3 us
  transfers between devices with their start and end apart: 10, of which 9 were waited for; matrix products, arithmetic and copies ran while one was open for 6% of the time, Pallas kernels for 0%

commit v1 on v0

--- a/solution.py
+++ b/solution.py
@@ -222,8 +222,11 @@
     )
     modulation_share = jnp.dot(onehot.T, grad_modrows, precision=PRECISE)
     summed = lax.psum(
-        (query_share, keyval_share, output_share, modulation_share, jnp.sum(grad_out, axis=0)),
-        ("rows", "mlp"),
+        lax.psum(
+            (query_share, keyval_share, output_share, modulation_share, jnp.sum(grad_out, axis=0)),
+            "mlp",
+        ),
+        "rows",
     )
     grad_query_weight, grad_keyval_weight, grad_out_weight, grad_modulation, grad_down_bias = summed
     grad_ada_weight = jnp.dot(noise_cond.astype(jnp.float32).T, grad_modulation, precision=PRECISE)

time: 822 us -> 855 us (1.040)
  waiting for transfers between devices: 357 us -> 446 us
  blocking collectives: 94.4 us -> 40 us
    psum x1, waiting for transfers between devices: 67.5 us -> 128 us  [shards(): lax.psum((query_share, keyval_share, output_share, modulation_share, jnp....]
    psum x1, blocking collectives: 37.3 us -> 5.07 us  [shards(): lax.psum((query_share, keyval_share, output_share, modulation_share, jnp....]
    psum x1, waiting for transfers between devices: 109 us -> 138 us  [shards(): lax.psum(lax.psum((query_share, keyval_share, output_share, modulation_sh...]
    psum x1, blocking collectives: 57.1 us -> 34.9 us  [shards(): lax.psum((up_share, upb_share, down_share), 'rows')]
    unnamed x81 -> x83, local copies, waits for them, and re-layouts: 55.4 us -> 53.6 us
  transfers between devices with their start and end apart: 10 -> 10, of which waited for: 9 -> 9; matrix products, arithmetic and copies ran while one was open for 6% -> 5% of each run, Pallas kernels for 0% -> 0%
where the time goes in v1:
time: 855 us; the launch traced here: 850 us
  waiting for transfers between devices  446 us (52%)
  other arithmetic  142 us (17%)
  local copies, waits for them, and re-layouts  141 us (16%)
  matrix products  55.6 us (7%)
  blocking collectives  40 us (5%)
  between operations  14.9 us (2%)
  starting transfers between devices  11.3 us (1%)
    psum x1, waiting for transfers between devices, shards(): lax.psum(lax.psum((query_share, keyval_share, output_share, modulation_sh...  138 us
    psum x1, waiting for transfers between devices, shards(): lax.psum((query_share, keyval_share, output_share, modulation_share, jnp....  128 us
    scatter-add x1, other arithmetic, attend_back(): table_grad.at[index_part.reshape(-1)]  72.1 us
    ppermute x2, waiting for transfers between devices, shifted(): return lax.ppermute(x, axis, [(i, (i + by) % peers) for i in range(peers)])  56.3 us
    unnamed x83, local copies, waits for them, and re-layouts  53.6 us
    gather x1, local copies, waits for them, and re-layouts, attend(): kv_table[index_part]  42.8 us
    dot_general x16, matrix products, bf_dot(): jnp.dot(left_operand, right_operand, preferred_element_type=jnp.float32)  35.4 us
    psum x1, blocking collectives, shards(): lax.psum((up_share, upb_share, down_share), 'rows')  34.9 us
  transfers between devices with their start and end apart: 10, of which 9 were waited for; matrix products, arithmetic and copies ran while one was open for 5% of the time, Pallas kernels for 0%

profile of v1, /device:TPU:0, one launch (start us, length us, event | category | flops | bytes accessed | tf_op | source)
XLA Modules:
  0.0 850.5 jit_solution(10976372186539591415)
XLA Ops:
  18.6 6.4 collective-permute-start.1
  26.4 29.9 %collective-permute-done.1 = bf16[512,1024]{1,0:T(8,128)(2,1)} collective-permute-done((bf16[512,1024]{1,0:T(8,128)(2,1)}, bf16[512,1024]{1,0:T(8,128)(2,1)}, u32[]{:S(2)}, u32[]{:S(2)}) %collective-permute-start.1) | collective-permute-done | bytes 1048608 | tf_op jit(solution)/shard_map/ppermute | solution.py:20
  60.4 42.8 %gather_fusion = bf16[8192,1024]{1,0:T(8,128)(2,1)} fusion(bf16[1536,1024]{1,0:T(8,128)(2,1)} %pad_maximum_fusion, s32[8192]{0:T(1024)S(1)} %broadcast_clamp_fusion), kind=kCustom, calls=%fused_computation | custom fusion | bytes 33587200 | tf_op jit(solution)/shard_map/while/body/eval_jaxpr/gather | solution.py:106
  103.2 18.5 %slice_bitcast_fusion.1 = (bf16[512,2,4,8,128]{4,3,2,1,0:T(8,128)(2,1)}, bf16[512,2,4,8,128]{4,3,2,1,0:T(8,128)(2,1)}, bf16[512,16,512]{2,1,0:T(8,128)(2,1)}, bf16[512,16,512]{2,1,0:T(8,128)(2,1)}) fusion(bf16[512,16,1024]{2,1,0:T(8,128)(2,1)} %bitcast.86), kind=kLoop, calls=%fused_computation.125 | loop fusion | bytes 50331648
  121.6 12.6 %reshape.162 = bf16[512,16,4,128]{3,2,1,0:T(4,128)(2,1)} reshape(bf16[512,16,512]{2,1,0:T(8,128)(2,1)} %get-tuple-element.110) | data formatting | bytes 16777216 | tf_op jit(solution)/shard_map/while/body/eval_jaxpr/reshape | solution.py:51
  134.2 13.0 %multiply_reduce_fusion.1 = f32[512,4,16]{1,2,0:T(8,128)} fusion(f32[512,4,128]{2,1,0:T(4,128)S(1)} %copy.76, bf16[512,16,4,128]{3,2,1,0:T(4,128)(2,1)} %reshape.162), kind=kLoop, calls=%fused_computation.10 | loop fusion | flops 12550144 | bytes 9568256
  151.0 5.7 fusion.8
  161.4 32.0 %all-gather.3.cloned.1.call-done = bf16[1024,512]{1,0:T(8,128)(2,1)} async-done(((bf16[512,512]{1,0:T(8,128)(2,1)}), bf16[1024,512]{1,0:T(8,128)(2,1)}) %all-gather.3.cloned.1.call-update) | async-done | bytes 1048592 | tf_op jit(solution)/shard_map/all_gather | solution.py:133
  193.3 5.5 multiply_convert_fusion.1
  198.8 17.4 %all-gather.5.cloned.1.call-done = bf16[1024,512]{1,0:T(8,128)(2,1)} async-done(((bf16[512,512]{1,0:T(8,128)(2,1)}), bf16[1024,512]{1,0:T(8,128)(2,1)}) %all-gather.5.cloned.1.call-update) | async-done | bytes 1048592 | tf_op jit(solution)/shard_map/all_gather | solution.py:139
  216.2 5.1 convert_reduce_fusion
  233.9 12.6 %reshape.163 = bf16[512,16,4,128]{3,2,1,0:T(4,128)(2,1)} reshape(bf16[512,16,512]{2,1,0:T(8,128)(2,1)} %get-tuple-element.111) | data formatting | bytes 16777216 | tf_op jit(solution)/shard_map/while/body/eval_jaxpr/reshape | solution.py:52
  246.5 10.8 %reduce-scatter.5.cloned.1.call-done = f32[512,512]{1,0:T(8,128)} async-done(((f32[1024,512]{1,0:T(8,128)}), f32[512,512]{1,0:T(8,128)}) %reduce-scatter.5.cloned.1.call-update) | async-done | bytes 1048592 | tf_op jit(solution)/shard_map/reduce_scatter | solution.py:141
  259.2 32.6 %reduce-scatter.3.cloned.1.call-done = f32[512,512]{1,0:T(8,128)} async-done(((f32[1024,512]{1,0:T(8,128)}), f32[512,512]{1,0:T(8,128)}) %reduce-scatter.3.cloned.1.call-update) | async-done | bytes 1048592 | tf_op jit(solution)/shard_map/reduce_scatter | solution.py:136
  299.2 24.5 %broadcast_multiply_fusion = (f32[512,4,128,16]{2,1,3,0:T(4,128)}, f32[512,4,16]{1,2,0:T(8,128)}) fusion(f32[512,4,128]{2,1,0:T(4,128)S(1)} %copy.77, f32[512,4,16]{1,2,0:T(8,128)} %copy.50, bf16[512,16,4,128]{3,2,1,0:T(4,128)(2,1)} %reshape.163), kind=kLoop, calls=%fused_computation.18 | loop fusion | flops 16744448 | bytes 26476544 | tf_op jit(solution)/shard_map/while/body/eval_jaxpr/bhj,bhe->bjhe/dot_general | solution.py:183
  323.6 12.7 %copy.114 = f32[1024,8,4,128]{3,1,2,0:T(8,128)} copy(f32[1024,8,4,128]{3,2,1,0:T(4,128)} %bitcast.88) | data formatting | bytes 33554432
  342.4 11.0 %multiply_multiply_fusion = f32[512,4,128,16]{2,1,3,0:T(4,128)S(1)} fusion(f32[512,4,128]{2,1,0:T(4,128)S(1)} %copy-done.7, f32[512,4,16]{1,2,0:T(8,128)} %copy.48), kind=kLoop, calls=%fused_computation.11 | loop fusion | flops 8388608 | bytes 17956864 | tf_op jit(solution)/shard_map/while/body/eval_jaxpr/mul | solution.py:180
  353.5 7.1 copy.115
  360.6 72.1 %scatter_custom_fusion = f32[1536,1024]{1,0:T(8,128)} fusion(s32[8192]{0:T(1024)S(1)} %bitcast.100, f32[8192,512]{1,0:T(8,128)} %bitcast.87, f32[]{:T(128)} %constant.96.clone.1, f32[8192,512]{1,0:T(8,128)} %bitcast.89, f32[]{:T(128)} %constant.55.clone.1), kind=kCustom, calls=%fused_computation.3 | custom fusion | flops 16777216 | bytes 39845896 | tf_op jit(solution)/shard_map/while/body/eval_jaxpr/scatter-add | solution.py:193
  442.0 5.8 fusion.5
  451.5 56.3 %collective-permute-done.2 = f32[512,1024]{1,0:T(8,128)} collective-permute-done((f32[512,1024]{1,0:T(8,128)}, f32[512,1024]{1,0:T(8,128)}, u32[]{:S(2)}, u32[]{:S(2)}) %collective-permute-start.2) | collective-permute-done | bytes 2097184 | tf_op jit(solution)/shard_map/ppermute | solution.py:27
  523.5 127.7 %all-reduce.8.cloned.1.call-done = (f32[8,2048]{1,0:T(8,128)}, f32[512,512]{1,0:T(8,128)}, f32[512,1024]{1,0:T(8,128)}, f32[512,512]{1,0:T(8,128)}) async-done(((f32[8,2048]{1,0:T(8,128)}, f32[512,512]{1,0:T(8,128)}, f32[512,1024]{1,0:T(8,128)}, f32[512,512]{1,0:T(8,128)}), (f32[8,2048]{1,0:T(8,128)}, f32[512,512]{1,0:T(8,128)}, f32[512,1024]{1,0:T(8,128)}, ...) | async-done | bytes 4259856 | tf_op jit(solution)/shard_map/psum | solution.py:225
  656.3 34.9 %all-reduce = (f32[1024]{0:T(1024)}, f32[512]{0:T(512)}) all-reduce(f32[1024]{0:T(1024)S(1)} %get-tuple-element.129, f32[512]{0:T(512)S(1)} %psum.102), channel_id=1, replica_groups=mesh['rows'=16,'mlp'=2] {'rows'}, use_global_device_ids=true, to_apply=%region_25.26 | all-reduce | flops 1536 | bytes 12288 | tf_op jit(solution)/shard_map/psum | solution.py:147
  691.2 138.1 %all-reduce.6.cloned.1.call-done = (f32[8,2048]{1,0:T(8,128)}, f32[512,512]{1,0:T(8,128)}, f32[512,1024]{1,0:T(8,128)}, f32[512,512]{1,0:T(8,128)}, f32[512,1024]{1,0:T(8,128)}, /*index=5*/f32[1024,512]{1,0:T(8,128)}) async-done(((f32[8,2048]{1,0:T(8,128)}, f32[512,512]{1,0:T(8,128)}, f32[512,1024]{1,0:T(8,128)}, f32[512,512]{1,0:T(8,128)}, f32[512,1024]{1,0:T(8,128)}, /*index=5*/f32[1024,512]{1,0:T(8,128)}), ...) | async-done | bytes 8454160 | tf_op jit(solution)/shard_map/psum | solution.py:224
  (158 shorter events, 100.7 us)
Async XLA Ops:
  7.2 186.2 %copy-start = (bf16[512,1024]{1,0:T(8,128)(2,1)S(1)}, bf16[512,1024]{1,0:T(8,128)(2,1)}, u32[]{:S(2)}) copy-start(bf16[512,1024]{1,0:T(8,128)(2,1)} %param.23) | copy-start | bytes 3145732
  7.2 9.4 %copy-start.5 = (bf16[512,512]{1,0:T(8,128)(2,1)S(1)}, bf16[512,512]{1,0:T(8,128)(2,1)}, u32[]{:S(2)}) copy-start(bf16[512,512]{1,0:T(8,128)(2,1)} %param.14) | copy-start | bytes 1572868
  7.2 186.1 %all-gather.3.cloned.1.call-start = ((), (), s32[]{:S(2)}) async-start(), calls=%async_computation.2 | async-start | bytes 1572864 | tf_op jit(solution)/shard_map/all_gather | solution.py:133
  10.0 8.6 %copy-start.27 = (f32[512]{0:T(512)}, f32[512]{0:T(512)S(1)}, u32[]{:S(2)}) copy-start(f32[512]{0:T(512)S(1)} %add_rsqrt_fusion.1) | copy-start | bytes 6148
  12.0 13.3 %copy-start.29 = (s32[512,16]{0,1:T(8,128)S(1)}, s32[512,16]{0,1:T(8,128)}, u32[]{:S(2)}) copy-start(s32[512,16]{0,1:T(8,128)} %param.17) | copy-start | bytes 98308
  16.6 9.0 %copy-start.17 = (bf16[512,512]{1,0:T(8,128)(2,1)S(1)}, bf16[512,512]{1,0:T(8,128)(2,1)}, u32[]{:S(2)}) copy-start(bf16[512,512]{1,0:T(8,128)(2,1)} %param.20) | copy-start | bytes 1572868
  16.9 9.2 %copy-start.8 = (bf16[512,512]{1,0:T(8,128)(2,1)}, bf16[512,512]{1,0:T(8,128)(2,1)S(1)}, u32[]{:S(2)}) copy-start(bf16[512,512]{1,0:T(8,128)(2,1)S(1)} %fusion.32) | copy-start | bytes 1572868
  18.6 37.7 %collective-permute-start.1 = (bf16[512,1024]{1,0:T(8,128)(2,1)}, bf16[512,1024]{1,0:T(8,128)(2,1)}, u32[]{:S(2)}, u32[]{:S(2)}) collective-permute-start(bf16[512,1024]{1,0:T(8,128)(2,1)} %convolution_convert_fusion), channel_id=1, source_target_pairs={{1,0},{2,1},{3,2},{4,3},{5,4},{6,5},{7,6},{8,7},{9,8},{10,9},{11,1... | collective-permute-start | bytes 3145736 | tf_op jit(solution)/shard_map/ppermute | solution.py:20
  25.0 32.2 %collective-permute-start = (bf16[512,1024]{1,0:T(8,128)(2,1)}, bf16[512,1024]{1,0:T(8,128)(2,1)}, u32[]{:S(2)}, u32[]{:S(2)}) collective-permute-start(bf16[512,1024]{1,0:T(8,128)(2,1)} %convolution_convert_fusion), channel_id=1, source_target_pairs={{0,1},{1,2},{2,3},{3,4},{4,5},{5,6},{6,7},{7,8},{8,9},{9,10},{10,1... | collective-permute-start | bytes 3145736 | tf_op jit(solution)/shard_map/ppermute | solution.py:19
  26.4 107.8 %copy-start.6 = (f32[512,4,128]{2,1,0:T(4,128)}, f32[512,4,128]{2,1,0:T(4,128)S(1)}, u32[]{:S(2)}) copy-start(f32[512,4,128]{2,1,0:T(4,128)S(1)} %copy.76) | copy-start | bytes 3145732
  160.0 56.2 %all-gather.5.cloned.1.call-start = ((), (), s32[]{:S(2)}) async-start(), calls=%async_computation.4 | async-start | bytes 1572864 | tf_op jit(solution)/shard_map/all_gather | solution.py:139
  160.8 96.5 %reduce-scatter.5.cloned.1.call-start = ((), (), s32[]{:S(2)}) async-start(), calls=%async_computation.5 | async-start | bytes 3145728 | tf_op jit(solution)/shard_map/reduce_scatter | solution.py:141
  225.3 66.6 %reduce-scatter.3.cloned.1.call-start = ((), (), s32[]{:S(2)}) async-start(), calls=%async_computation.3 | async-start | bytes 3145728 | tf_op jit(solution)/shard_map/reduce_scatter | solution.py:136
  229.8 421.4 %all-reduce.8.cloned.1.call-start = ((), (), s32[]{:S(2)}) async-start(), calls=%async_computation.7 | async-start | bytes 8519680 | tf_op jit(solution)/shard_map/psum | solution.py:225
  437.6 70.2 %collective-permute-start.2 = (f32[512,1024]{1,0:T(8,128)}, f32[512,1024]{1,0:T(8,128)}, u32[]{:S(2)}, u32[]{:S(2)}) collective-permute-start(f32[512,1024]{1,0:T(8,128)} %get-tuple-element.112), channel_id=1, source_target_pairs={{0,31},{1,0},{2,1},{3,2},{4,3},{5,4},{6,5},{7,6},{8,7},{9,8},{10,9... | collective-permute-start | bytes 6291464 | tf_op jit(solution)/shard_map/ppermute | solution.py:27
  441.3 66.5 %collective-permute-start.3 = (f32[512,1024]{1,0:T(8,128)}, f32[512,1024]{1,0:T(8,128)}, u32[]{:S(2)}, u32[]{:S(2)}) collective-permute-start(f32[512,1024]{1,0:T(8,128)} %get-tuple-element.113), channel_id=1, source_target_pairs={{0,1},{1,2},{2,3},{3,4},{4,5},{5,6},{6,7},{7,8},{8,9},{9,10},{10,1... | collective-permute-start | bytes 6291464 | tf_op jit(solution)/shard_map/ppermute | solution.py:27
  451.5 61.8 %copy-start.4 = (f32[512,2048]{1,0:T(8,128)S(1)}, f32[512,2048]{1,0:T(8,128)}, u32[]{:S(2)}) copy-start(f32[512,2048]{1,0:T(8,128)} %copy-done.2) | copy-start | bytes 12582916
  451.5 61.8 %copy-start.23 = (bf16[512,1024]{1,0:T(8,128)(2,1)S(1)}, bf16[512,1024]{1,0:T(8,128)(2,1)}, u32[]{:S(2)}) copy-start(bf16[512,1024]{1,0:T(8,128)(2,1)} %param.21) | copy-start | bytes 3145732
  451.5 61.8 %copy-start.26 = (f32[512]{0:T(512)S(1)}, f32[512]{0:T(512)}, u32[]{:S(2)}) copy-start(f32[512]{0:T(512)} %copy-done.25) | copy-start | bytes 6148
  451.5 61.8 %copy-start.28 = (f32[512]{0:T(512)S(1)}, f32[512]{0:T(512)}, u32[]{:S(2)}) copy-start(f32[512]{0:T(512)} %copy-done.27) | copy-start | bytes 6148
  518.3 311.1 %all-reduce.6.cloned.1.call-start = ((), (), s32[]{:S(2)}) async-start(), calls=%async_computation.6 | async-start | bytes 16908288 | tf_op jit(solution)/shard_map/psum | solution.py:224
  651.2 178.1 %copy-start.11 = (bf16[128,2048]{1,0:T(8,128)(2,1)S(1)}, bf16[128,2048]{1,0:T(8,128)(2,1)}, u32[]{:S(2)}) copy-start(bf16[128,2048]{1,0:T(8,128)(2,1)} %param.18) | copy-start | bytes 1572868
  651.2 181.7 %copy-start.30 = (bf16[8,128]{1,0:T(8,128)(2,1)S(1)}, bf16[8,128]{1,0:T(8,128)(2,1)}, u32[]{:S(2)}) copy-start(bf16[8,128]{1,0:T(8,128)(2,1)} %param.15) | copy-start | bytes 6148
  829.3 9.1 %copy-start.16 = (f32[512,1024]{1,0:T(8,128)S(1)}, f32[512,1024]{1,0:T(8,128)}, u32[]{:S(2)}) copy-start(f32[512,1024]{1,0:T(8,128)} %get-tuple-element.139) | copy-start | bytes 6291460
  (22 other events, 86.2 us)
Sparse Core Ops, SparseCore 0:
  160.1 33.1 all-gather.2
  194.9 21.2 all-gather.4
  225.4 31.8 reduce-scatter.4
  260.0 31.8 reduce-scatter.2
  518.4 132.7 all-reduce.7
  656.7 172.6 all-reduce.5
